TPU v7x, 32 devices: a whole 2x2x4 slice. The times are simulated.
32 devices in a mesh: groups: 2 (over y), sect: 4 (over x, core), hid: 4 (over z).
Axes of the slice: x: 2, y: 2, z: 4, core: 2. Of those that a mesh axis runs over, the one named last changes fastest.
Arguments:
- resid: bfloat16 [1024, 4096], P(('groups', 'sect'), 'hid'), parts along dimension 0, may hold values from -64 to 64
- moe_gain: bfloat16 [4096], replicated, may hold values from 0.25 to 1.75
- routes: int32 [1024, 2], P(('groups', 'sect')), parts along dimension 0, may hold values from 0 to 3, all different within a row; in each aligned block of 128 rows (0 to 127, 128 to 255, ...) at most 128 rows name the same one
- gate_q: int32 [1024, 2], P(('groups', 'sect')), parts along dimension 0, may hold values from 16 to 255
- doc_lengths: int32 [8, 4], P(('groups', 'sect')), parts along dimension 0, may hold values from 1 to 64, 128 in all within a row
- w_gate: bfloat16 [4, 4096, 4096], P('sect', None, 'hid'), may hold values from -0.09375 to 0.09375
- w_up: bfloat16 [4, 4096, 4096], P('sect', None, 'hid'), may hold values from -0.09375 to 0.09375
- w_down: bfloat16 [4, 4096, 4096], P('sect', 'hid'), may hold values from -0.09375 to 0.09375
- attn_gain: bfloat16 [4096], replicated, may hold values from 0.25 to 1.75
- w_q: bfloat16 [4096, 4096], P('sect', 'hid')
- w_k: bfloat16 [4096, 1024], P('sect', 'hid')
- w_v: bfloat16 [4096, 1024], P('sect', 'hid'), may hold values from -0.09375 to 0.09375
Outputs:
- new_resid: bfloat16 [1024, 4096], P(('groups', 'sect'), 'hid'), parts along dimension 0
- context: bfloat16 [1024, 4096], P(('groups', 'sect'), 'hid'), parts along dimension 0
There are 2 independent parts, one for each index of `groups`. A program takes and returns all parts, laid end to end along the dimension named above; an argument that names none is the same for every part. Nothing has to cross between parts.
Inputs may be any that keep to these rules, and one draw needn't show every extreme that they name: `routes`: within the rows of one index of sect (aligned blocks of 128 rows) no expert is named by more than 128 rows. `doc_lengths`: each row sums to 128.
All inputs are finite; a program needn't handle non-finite values.
Results may differ from a plain program's by a relative error of at most 0.012.
The roundings to bfloat16 on the way count: a program that leaves them out, or rounds other values in their place, can miss the bound.
Values may be sent and summed in bfloat16 or wider, within the bound.
No kernel may reach another device: no remote copies, remote signals or barrier semaphores. Data moves between devices by JAX's collectives and lax.ppermute only.
A program may use at most 128 MiB of HBM per device.

v0:
```python
import math
import jax
import jax.numpy as jnp
from jax import lax
from jax.sharding import PartitionSpec as P

H = 32
KVH = 8
HD = 128


def layer_norm(values, gain):
    center = values - jnp.mean(values, axis=1, keepdims=True)
    spread = jnp.mean(center * center, axis=1, keepdims=True)
    return (center * lax.rsqrt(spread + 1e-05) * gain.astype(jnp.float32)).astype(jnp.bfloat16)


def slot_targets(route_rows, experts, capacity):
    flat = route_rows.reshape(-1)
    onehot = (flat[:, None] == jnp.arange(experts, dtype=jnp.int32)[None, :]).astype(jnp.int32)
    before = jnp.cumsum(onehot, axis=0, dtype=jnp.int32) - onehot
    return flat * capacity + jnp.sum(before * onehot, axis=1, dtype=jnp.int32)


def source_rows(targets, experts, capacity):
    count = targets.shape[0]
    filler = jnp.full((experts * capacity,), count, jnp.int32)
    return filler.at[targets].set(jnp.arange(count, dtype=jnp.int32)) // 2


def rotate(values, position, head):
    count = values.shape[0]
    split_heads = values.reshape(count, -1, head)
    half = head // 2
    freqs = jnp.exp(jnp.arange(half, dtype=jnp.float32) * (-2.0 * math.log(10000.0) / head))
    angles = position[:, None, None] * freqs[None, None, :]
    cosine = jnp.cos(angles)
    sine = jnp.sin(angles)
    first = split_heads[:, :, :half]
    second = split_heads[:, :, half:]
    turned = jnp.concatenate(
        [first * cosine - second * sine, second * cosine + first * sine], axis=2
    )
    return turned.reshape(count, -1)


def attend(query, keys, vals, lengths, head, group):
    count = query.shape[0]
    kv_heads = keys.shape[1] // head
    ends = jnp.cumsum(lengths, dtype=jnp.int32)
    places = jnp.arange(count, dtype=jnp.int32)
    after = (places[:, None] >= ends[None, :]).astype(jnp.int32)
    doc_ids = jnp.sum(after, axis=1, dtype=jnp.int32)
    starts = jnp.sum(after * lengths[None, :], axis=1, dtype=jnp.int32)
    position = (places - starts).astype(jnp.float32)
    rotated_q = (
        rotate(query, position, head).astype(jnp.bfloat16).reshape(count, kv_heads, group, head)
    )
    rotated_k = rotate(keys, position, head).astype(jnp.bfloat16).reshape(count, kv_heads, head)
    value_heads = vals.reshape(count, kv_heads, head)
    allowed = (doc_ids[:, None] == doc_ids[None, :]) & (places[None, :] <= places[:, None])
    scores = jnp.einsum(
        "tkgd,skd->kgts", rotated_q, rotated_k, preferred_element_type=jnp.float32
    ) * (1.0 / math.sqrt(head))
    scores = jnp.where(allowed[None, None], scores, -jnp.inf)
    highest = jnp.max(scores, axis=3, keepdims=True)
    weights = jnp.exp(scores - highest)
    probs = (weights / jnp.sum(weights, axis=3, keepdims=True)).astype(jnp.bfloat16)
    mixed = jnp.einsum("kgts,skd->tkgd", probs, value_heads, preferred_element_type=jnp.float32)
    return mixed.astype(jnp.bfloat16).reshape(count, -1)


def on_device(
    resid, moe_gain, routes, gate_q, doc_lengths, w_gate, w_up, w_down, attn_gain, w_q, w_k, w_v
):
    sections = lax.axis_size("sect")
    slices = lax.axis_size("hid")
    tokens_here, local_width = resid.shape
    width = local_width * slices
    capacity = 4 * tokens_here // sections
    entry = lax.all_gather(resid, "hid", axis=1, tiled=True)
    normed = layer_norm(entry.astype(jnp.float32), moe_gain)
    targets = slot_targets(routes, sections, capacity)
    sources = source_rows(targets, sections, capacity)
    padded = jnp.concatenate([normed, jnp.zeros((1, width), jnp.bfloat16)], axis=0)
    gate_w = w_gate[0]
    up_w = w_up[0]
    down_w = w_down[0]
    outgoing = padded[sources].reshape(sections, capacity, width)
    arrived = lax.all_to_all(outgoing, "sect", split_axis=0, concat_axis=0, tiled=True).reshape(
        sections * capacity, width
    )
    gate = jnp.dot(arrived, gate_w, preferred_element_type=jnp.float32)
    up = jnp.dot(arrived, up_w, preferred_element_type=jnp.float32)
    hidden = (jax.nn.silu(gate) * up).astype(jnp.bfloat16)
    weights = gate_q.reshape(-1).astype(jnp.float32) / 256.0
    own_resid = resid.astype(jnp.float32)
    outputs = jnp.dot(hidden, down_w, preferred_element_type=jnp.float32)
    mine = lax.psum_scatter(outputs, "hid", scatter_dimension=1, tiled=True)
    returned = lax.all_to_all(
        mine.reshape(sections, capacity, local_width),
        "sect",
        split_axis=0,
        concat_axis=0,
        tiled=True,
    )
    picked = returned.reshape(sections * capacity, local_width)[targets]
    mixture = jnp.sum((picked * weights[:, None]).reshape(tokens_here, 2, local_width), axis=1)
    new_local = (own_resid + mixture).astype(jnp.bfloat16)
    full_rows = lax.all_gather(new_local, "hid", axis=1, tiled=True)
    normed_next = layer_norm(full_rows.astype(jnp.float32), attn_gain)
    query = jnp.dot(
        normed_next,
        lax.all_gather(w_q, "sect", axis=0, tiled=True),
        preferred_element_type=jnp.float32,
    )
    keys = jnp.dot(
        normed_next,
        lax.all_gather(w_k, "sect", axis=0, tiled=True),
        preferred_element_type=jnp.float32,
    )
    vals = jnp.dot(
        normed_next,
        lax.all_gather(w_v, "sect", axis=0, tiled=True),
        preferred_element_type=jnp.float32,
    )
    context = attend(query, keys, vals.astype(jnp.bfloat16), doc_lengths[0], HD, H // KVH)
    return (new_local, context)


def solution(mesh):
    in_specs = (
        P(("groups", "sect"), "hid"),
        P(),
        P(("groups", "sect"), None),
        P(("groups", "sect"), None),
        P(("groups", "sect"), None),
        P("sect", None, "hid"),
        P("sect", None, "hid"),
        P("sect", "hid", None),
        P(),
        P("sect", "hid"),
        P("sect", "hid"),
        P("sect", "hid"),
    )
    out_specs = (P(("groups", "sect"), "hid"), P(("groups", "sect"), "hid"))
    return jax.shard_map(
        on_device, mesh=mesh, in_specs=in_specs, out_specs=out_specs, check_vma=False
    )
```

profile of v0, /device:TPU:0, one launch (start us, length us, event | category | flops | bytes accessed | tf_op | source)
XLA Modules:
  0.0 450.2 jit_solution(11100007344031387848)
XLA Ops:
  7.2 0.0 all-gather.6.cloned.1.call-start
  7.2 0.7 all-gather.6.cloned.1.call-update
  7.9 0.0 reduce-scatter.2.cloned.1.call-start
  7.9 0.8 copy.36
  8.7 0.1 eq.46
  8.9 0.1 eq.42
  9.0 0.7 convert_element_type.72
  9.7 1.2 reduce-window.18
  10.9 0.1 slice.28
  11.0 0.1 copy.38
  11.2 0.1 copy.39
  11.2 0.7 broadcast_multiply_fusion
  11.9 0.1 copy.35
  12.0 0.1 mul.191
  12.2 0.1 add_bitcast_fusion
  12.3 1.4 scatter_custom_fusion
  13.7 26.5 %all-gather.6.cloned.1.call-done = bf16[128,4096]{1,0:T(8,128)(2,1)} async-done(((bf16[128,1024]{1,0:T(8,128)(2,1)}), bf16[128,4096]{1,0:T(8,128)(2,1)}) %all-gather.6.cloned.1.call-update) | async-done | bytes 1048592 | tf_op jit(solution)/shard_map/all_gather | solution.py:81
  40.2 1.5 convert_reduce_fusion.1
  41.8 1.7 fusion.14
  43.5 0.4 fusion.16
  43.9 0.1 concatenate.11
  44.0 4.4 gather_fusion
  48.3 51.9 %all_to_all.10 = bf16[4,128,4096]{2,1,0:T(8,128)(2,1)S(1)} all-to-all(bf16[4,128,4096]{2,1,0:T(8,128)(2,1)} %bitcast.87), channel_id=1, replica_groups=mesh['groups'=2,'sect'=4,'hid'=4] {'sect'}, dimensions={0} | all-to-all | bytes 8388608 | tf_op jit(solution)/shard_map/all_to_all | solution.py:90
  100.2 2.0 copy-done.1
  102.2 6.9 %fusion.5 = f32[512,1024]{1,0:T(8,128)S(1)} fusion(bf16[512,4096]{1,0:T(8,128)(2,1)S(1)} %bitcast.89, bf16[1,4096,1024]{2,1,0:T(8,128)(2,1)} %param.17), kind=kOutput, calls=%fused_computation.8 | convolution fusion | flops 4294967296 | bytes 14680064 | tf_op jit(solution)/shard_map/dot_general | solution.py:93
  109.1 19.1 %fusion.1 = f32[512,4096]{1,0:T(8,128)} fusion(bf16[1,1024,4096]{2,1,0:T(8,128)(2,1)} %param.19, f32[512,1024]{1,0:T(8,128)S(1)} %fusion.5, bf16[512,4096]{1,0:T(8,128)(2,1)} %bitcast.90, bf16[1,4096,1024]{2,1,0:T(8,128)(2,1)} %param.18), kind=kOutput, calls=%fused_computation.4 | convolution fusion | flops 8593080320 | bytes 31457280 | tf_op jit(solution)/shard_map/dot_general | solution.py:98
  128.2 143.2 %reduce-scatter.2.cloned.1.call-done = f32[512,1024]{1,0:T(8,128)} async-done(((f32[512,4096]{1,0:T(8,128)}), f32[512,1024]{1,0:T(8,128)}) %reduce-scatter.2.cloned.1.call-update) | async-done | bytes 2097168 | tf_op jit(solution)/shard_map/reduce_scatter | solution.py:99
  271.4 3.7 all-to-all-start.1
  275.2 0.2 all-gather.8.cloned.1.call-start
  275.4 0.1 copy.40
  275.5 25.3 %all-to-all-done.1 = f32[4,128,1024]{2,1,0:T(8,128)S(1)} async-done(((f32[4,128,1024]{2,1,0:T(8,128)}), f32[4,128,1024]{2,1,0:T(8,128)S(1)}, u32[]{:S(2)}, u32[]{:S(2)}) %all-to-all-start.1) | async-done | bytes 2097184 | tf_op jit(solution)/shard_map/all_to_all | solution.py:100
  300.8 1.1 gather_fusion.1
  301.9 0.6 gather.10
  302.6 1.3 multiply_reduce_fusion
  303.9 0.8 add_convert_fusion.1
  304.7 0.0 all-gather.12.cloned.1.call-start
  304.8 0.5 all-gather.12.cloned.1.call-update
  305.3 0.0 all-gather.14.cloned.1.call-start
  305.4 0.5 all-gather.14.cloned.1.call-update
  305.9 0.0 all-gather.10.cloned.1.call-start
  306.0 0.5 all-gather.10.cloned.1.call-update
  306.5 0.2 reduce-window.20
  306.7 0.1 convert_reduce_fusion.2
  306.8 0.3 multiply_cosine_fusion
  307.1 0.1 fusion.25
  307.2 25.4 %all-gather.8.cloned.1.call-done = bf16[128,4096]{1,0:T(8,128)(2,1)} async-done(((bf16[128,1024]{1,0:T(8,128)(2,1)}), bf16[128,4096]{1,0:T(8,128)(2,1)}) %all-gather.8.cloned.1.call-update) | async-done | bytes 1048592 | tf_op jit(solution)/shard_map/all_gather | solution.py:110
  332.6 1.5 convert_reduce_fusion
  334.2 1.7 fusion.11
  335.9 20.3 %all-gather.12.cloned.1.call-done = bf16[4096,256]{1,0:T(8,128)(2,1)} async-done(((bf16[1024,256]{1,0:T(8,128)(2,1)}), bf16[4096,256]{1,0:T(8,128)(2,1)}) %all-gather.12.cloned.1.call-update) | async-done | bytes 2097168 | tf_op jit(solution)/shard_map/all_gather | solution.py:119
  356.2 2.1 fusion.40
  358.3 0.1 reshape.263
  358.4 57.5 %all-gather.14.cloned.1.call-done = bf16[4096,1024]{1,0:T(8,128)(2,1)} async-done(((bf16[1024,1024]{1,0:T(8,128)(2,1)}), bf16[4096,1024]{1,0:T(8,128)(2,1)}) %all-gather.14.cloned.1.call-update) | async-done | bytes 8388624 | tf_op jit(solution)/shard_map/all_gather | solution.py:114
  415.9 4.7 %convolution_bitcast_fusion = f32[16,8,8,128]{3,1,2,0:T(8,128)S(1)} fusion(bf16[4096,1024]{1,0:T(8,128)(2,1)} %all-gather.14.cloned.1.call-done, bf16[128,4096]{1,0:T(8,128)(2,1)S(1)} %copy-done.2, f32[4096]{0:T(1024)S(1)} %convert_element_type.80, f32[128]{0:T(128)S(1)} %add_rsqrt_fusion, f32[128]{0:T(128)S(1)} %broadcast_multiply_fusion.1), kind=kOutput, calls=%fused_computation.27 | convolution fusion | flops 1076363264 | bytes 9978880 | tf_op jit(solution)/shard_map/dot_general | solution.py:112
  420.6 0.1 copy.54
  420.7 0.3 subtract_convert_fusion
  421.0 0.1 pad_maximum_fusion
  421.2 0.2 fusion.43
  421.4 0.4 fusion.44
  421.8 0.3 fusion.22
  422.1 17.9 %all-gather.10.cloned.1.call-done = bf16[4096,256]{1,0:T(8,128)(2,1)} async-done(((bf16[1024,256]{1,0:T(8,128)(2,1)}), bf16[4096,256]{1,0:T(8,128)(2,1)}) %all-gather.10.cloned.1.call-update) | async-done | bytes 2097168 | tf_op jit(solution)/shard_map/all_gather | solution.py:124
  439.9 2.1 convolution_convert_fusion.1
  442.1 0.1 copy.50
  442.2 0.3 convolution_convert_fusion
  442.5 0.9 copy.46
  (34 shorter events, 0.3 us)
Async XLA Ops:
  7.2 33.1 %all-gather.6.cloned.1.call-start = ((), (), s32[]{:S(2)}) async-start(), calls=%async_computation.3 | async-start | bytes 1310720 | tf_op jit(solution)/shard_map/all_gather | solution.py:81
  7.9 263.5 %reduce-scatter.2.cloned.1.call-start = ((), (), s32[]{:S(2)}) async-start(), calls=%async_computation.4 | async-start | bytes 10485760 | tf_op jit(solution)/shard_map/reduce_scatter | solution.py:99
  40.2 3.2 copy-start
  100.2 2.0 copy-start.1
  271.4 4.0 copy-start.5
  271.4 29.4 %all-to-all-start.1 = ((f32[4,128,1024]{2,1,0:T(8,128)}), f32[4,128,1024]{2,1,0:T(8,128)S(1)}, u32[]{:S(2)}, u32[]{:S(2)}) async-start(f32[4,128,1024]{2,1,0:T(8,128)} %bitcast.91), calls=%async_computation.2 | async-start | bytes 4194304 | tf_op jit(solution)/shard_map/all_to_all | solution.py:100
  275.2 57.5 %all-gather.8.cloned.1.call-start = ((), (), s32[]{:S(2)}) async-start(), calls=%async_computation.5 | async-start | bytes 1310720 | tf_op jit(solution)/shard_map/all_gather | solution.py:110
  301.9 2.0 copy-start.3
  303.9 2.6 copy-start.4
  303.9 2.6 copy-start.6
  304.7 51.4 %all-gather.12.cloned.1.call-start = ((), (), s32[]{:S(2)}) async-start(), calls=%async_computation.7 | async-start | bytes 2621440 | tf_op jit(solution)/shard_map/all_gather | solution.py:119
  305.3 110.6 %all-gather.14.cloned.1.call-start = ((), (), s32[]{:S(2)}) async-start(), calls=%async_computation.8 | async-start | bytes 10485760 | tf_op jit(solution)/shard_map/all_gather | solution.py:114
  305.9 134.0 %all-gather.10.cloned.1.call-start = ((), (), s32[]{:S(2)}) async-start(), calls=%async_computation.6 | async-start | bytes 2621440 | tf_op jit(solution)/shard_map/all_gather | solution.py:124
  332.6 23.5 %copy-start.2 = (bf16[128,4096]{1,0:T(8,128)(2,1)S(1)}, bf16[128,4096]{1,0:T(8,128)(2,1)}, u32[]{:S(2)}) copy-start(bf16[128,4096]{1,0:T(8,128)(2,1)} %all-gather.8.cloned.1.call-done) | copy-start | bytes 3145732
Sparse Core Ops, SparseCore 0:
  9.6 30.6 all-gather.5
  128.3 143.0 reduce-scatter.1
  304.9 27.7 all-gather.7
  334.1 22.0 all-gather.11
  357.6 58.2 all-gather.13
  417.3 22.5 all-gather.9
where the time goes:
time: 451 us; the launch traced here: 450 us
  waiting for transfers between devices  318 us (71%)
  blocking collectives  51.9 us (12%)
  matrix products  35.8 us (8%)
  between operations  14.4 us (3%)
  other arithmetic  12.8 us (3%)
  local copies, waits for them, and re-layouts  12.6 us (3%)
    reduce_scatter x1, waiting for transfers between devices, on_device(): mine = lax.psum_scatter(outputs, 'hid', scatter_dimension=1, tiled=True)  143 us
    all_gather x1, waiting for transfers between devices, on_device(): lax.all_gather(w_q, 'sect', axis=0, tiled=True)  57.5 us
    all_to_all x1, blocking collectives, on_device(): lax.all_to_all(outgoing, 'sect', split_axis=0, concat_axis=0, tiled=True)  51.9 us
    all_gather x1, waiting for transfers between devices, on_device(): entry = lax.all_gather(resid, 'hid', axis=1, tiled=True)  26.5 us
    all_gather x1, waiting for transfers between devices, on_device(): full_rows = lax.all_gather(new_local, 'hid', axis=1, tiled=True)  25.4 us
    all_to_all x1, waiting for transfers between devices, on_device(): lax.all_to_all(mine.reshape(sections, capacity, local_width), 'sect', spl...  25.3 us
    all_gather x1, waiting for transfers between devices, on_device(): lax.all_gather(w_k, 'sect', axis=0, tiled=True)  20.3 us
    dot_general x1, matrix products, on_device(): outputs = jnp.dot(hidden, down_w, preferred_element_type=jnp.float32)  19.1 us
  transfers between devices with their start and end apart: 7, of which 7 were waited for; matrix products, arithmetic and copies ran while one was open for 4% of the time, Pallas kernels for 0%

commit v1 on v0

--- a/solution.py
+++ b/solution.py
@@ -107,7 +107,13 @@
     picked = returned.reshape(sections * capacity, local_width)[targets]
     mixture = jnp.sum((picked * weights[:, None]).reshape(tokens_here, 2, local_width), axis=1)
     new_local = (own_resid + mixture).astype(jnp.bfloat16)
-    full_rows = lax.all_gather(new_local, "hid", axis=1, tiled=True)
+    size = lax.axis_size("hid")
+    block, parts = (new_local, [new_local])
+    for _ in range(size - 1):
+        block = lax.ppermute(block, "hid", [(i, (i + 1) % size) for i in range(size)])
+        parts.insert(0, block)
+    line = jnp.concatenate(parts, axis=1)
+    full_rows = jnp.roll(line, (lax.axis_index("hid") + 1) * new_local.shape[1], axis=1)
     normed_next = layer_norm(full_rows.astype(jnp.float32), attn_gain)
     query = jnp.dot(
         normed_next,

time: 451 us -> 352 us (0.78)
  waiting for transfers between devices: 318 us -> 220 us
    all_gather x1, waiting for transfers between devices: 57.5 us -> 0.03 us  [on_device(): lax.all_gather(w_q, 'sect', axis=0, tiled=True)]
    all_gather x1 -> x0, waiting for transfers between devices: 25.4 us -> none  [on_device(): full_rows = lax.all_gather(new_local, 'hid', axis=1, tiled=True)]
    ppermute x0 -> x3, waiting for transfers between devices: none -> 24.6 us  [on_device(): lax.ppermute(block, 'hid', [(i, (i + 1) % size) for i in range(size)])]
    all_gather x1, waiting for transfers between devices: 20.3 us -> 0.03 us  [on_device(): lax.all_gather(w_k, 'sect', axis=0, tiled=True)]
    all_gather x1, waiting for transfers between devices: 17.9 us -> 0.03 us  [on_device(): lax.all_gather(w_v, 'sect', axis=0, tiled=True)]
  transfers between devices with their start and end apart: 7 -> 9, of which waited for: 7 -> 6; matrix products, arithmetic and copies ran while one was open for 4% -> 5% of each run, Pallas kernels for 0% -> 0%
where the time goes in v1:
time: 352 us
  waiting for transfers between devices  220 us (62%)
  blocking collectives  51.9 us (15%)
  matrix products  35.8 us (10%)
  between operations  16.1 us (5%)
  local copies, waits for them, and re-layouts  12.7 us (4%)
  other arithmetic  9.6 us (3%)
  starting transfers between devices  5.35 us (2%)
    reduce_scatter x1, waiting for transfers between devices, on_device(): mine = lax.psum_scatter(outputs, 'hid', scatter_dimension=1, tiled=True)  142 us
    all_to_all x1, blocking collectives, on_device(): lax.all_to_all(outgoing, 'sect', split_axis=0, concat_axis=0, tiled=True)  51.9 us
    all_gather x1, waiting for transfers between devices, on_device(): entry = lax.all_gather(resid, 'hid', axis=1, tiled=True)  26.5 us
    all_to_all x1, waiting for transfers between devices, on_device(): lax.all_to_all(mine.reshape(sections, capacity, local_width), 'sect', spl...  25.3 us
    ppermute x3, waiting for transfers between devices, on_device(): lax.ppermute(block, 'hid', [(i, (i + 1) % size) for i in range(size)])  24.6 us
    dot_general x1, matrix products, on_device(): outputs = jnp.dot(hidden, down_w, preferred_element_type=jnp.float32)  19.1 us
  transfers between devices with their start and end apart: 9, of which 6 were waited for; matrix products, arithmetic and copies ran while one was open for 5% of the time, Pallas kernels for 0%

profile of v1, /device:TPU:0, one launch (start us, length us, event | category | flops | bytes accessed | tf_op | source)
XLA Modules:
  0.0 351.8 jit_solution(8776761472502916845)
XLA Ops:
  8.0 0.0 all-gather.5.cloned.1.call-start
  8.0 0.7 all-gather.5.cloned.1.call-update
  8.7 0.0 reduce-scatter.2.cloned.1.call-start
  8.8 0.8 copy.36
  9.6 0.1 eq.49
  9.7 0.1 eq.45
  9.8 0.7 convert_element_type.72
  10.6 1.2 reduce-window.18
  11.8 0.1 slice.28
  11.8 0.1 copy.38
  12.0 0.1 copy.39
  12.1 0.7 broadcast_multiply_fusion
  12.8 0.1 copy.35
  12.9 0.1 mul.194
  13.0 0.1 add_bitcast_fusion
  13.1 1.4 scatter_custom_fusion
  14.6 26.5 %all-gather.5.cloned.1.call-done = bf16[128,4096]{1,0:T(8,128)(2,1)} async-done(((bf16[128,1024]{1,0:T(8,128)(2,1)}), bf16[128,4096]{1,0:T(8,128)(2,1)}) %all-gather.5.cloned.1.call-update) | async-done | bytes 1048592 | tf_op jit(solution)/shard_map/all_gather | solution.py:81
  41.1 1.5 convert_reduce_fusion.1
  42.6 1.7 fusion.14
  44.3 0.4 fusion.16
  44.7 0.1 concatenate.17
  44.8 4.4 %gather_fusion = bf16[512,4096]{1,0:T(8,128)(2,1)} fusion(bf16[129,4096]{1,0:T(8,128)(2,1)S(1)} %concatenate.17, s32[1024]{0:T(1024)S(1)} %pad_clamp_fusion.1), kind=kCustom, calls=%fused_computation | custom fusion | bytes 8390656 | tf_op jit(solution)/shard_map/gather | solution.py:89
  49.2 51.9 %all_to_all.10 = bf16[4,128,4096]{2,1,0:T(8,128)(2,1)S(1)} all-to-all(bf16[4,128,4096]{2,1,0:T(8,128)(2,1)} %bitcast.87), channel_id=1, replica_groups=mesh['groups'=2,'sect'=4,'hid'=4] {'sect'}, dimensions={0} | all-to-all | bytes 8388608 | tf_op jit(solution)/shard_map/all_to_all | solution.py:90
  101.1 1.9 copy-done.1
  103.0 6.9 %fusion.5 = f32[512,1024]{1,0:T(8,128)S(1)} fusion(bf16[512,4096]{1,0:T(8,128)(2,1)S(1)} %bitcast.89, bf16[1,4096,1024]{2,1,0:T(8,128)(2,1)} %param.17), kind=kOutput, calls=%fused_computation.8 | convolution fusion | flops 4294967296 | bytes 14680064 | tf_op jit(solution)/shard_map/dot_general | solution.py:93
  109.9 19.1 %fusion.1 = f32[512,4096]{1,0:T(8,128)} fusion(bf16[1,1024,4096]{2,1,0:T(8,128)(2,1)} %param.19, f32[512,1024]{1,0:T(8,128)S(1)} %fusion.5, bf16[512,4096]{1,0:T(8,128)(2,1)} %bitcast.90, bf16[1,4096,1024]{2,1,0:T(8,128)(2,1)} %param.18), kind=kOutput, calls=%fused_computation.4 | convolution fusion | flops 8593080320 | bytes 31457280 | tf_op jit(solution)/shard_map/dot_general | solution.py:98
  129.0 0.0 all-gather.9.cloned.1.call-start
  129.0 0.5 all-gather.9.cloned.1.call-update
  129.5 0.0 all-gather.11.cloned.1.call-start
  129.6 0.5 all-gather.11.cloned.1.call-update
  130.1 142.1 %reduce-scatter.2.cloned.1.call-done = f32[512,1024]{1,0:T(8,128)} async-done(((f32[512,4096]{1,0:T(8,128)}), f32[512,1024]{1,0:T(8,128)}) %reduce-scatter.2.cloned.1.call-update) | async-done | bytes 2097168 | tf_op jit(solution)/shard_map/reduce_scatter | solution.py:99
  272.2 3.7 %all-to-all-start.1 = ((f32[4,128,1024]{2,1,0:T(8,128)}), f32[4,128,1024]{2,1,0:T(8,128)S(1)}, u32[]{:S(2)}, u32[]{:S(2)}) async-start(f32[4,128,1024]{2,1,0:T(8,128)} %bitcast.91), calls=%async_computation.2 | async-start | bytes 4194304 | tf_op jit(solution)/shard_map/all_to_all | solution.py:100
  275.9 0.2 all-gather.7.cloned.1.call-start
  276.2 0.1 copy.40
  276.3 25.3 %all-to-all-done.1 = f32[4,128,1024]{2,1,0:T(8,128)S(1)} async-done(((f32[4,128,1024]{2,1,0:T(8,128)}), f32[4,128,1024]{2,1,0:T(8,128)S(1)}, u32[]{:S(2)}, u32[]{:S(2)}) %all-to-all-start.1) | async-done | bytes 2097184 | tf_op jit(solution)/shard_map/all_to_all | solution.py:100
  301.6 1.1 gather_fusion.1
  302.7 0.6 gather.10
  303.3 1.3 multiply_reduce_fusion
  304.7 0.1 add_convert_fusion.1
  304.8 1.2 collective-permute-start
  306.1 0.2 reduce-window.20
  306.2 0.1 convert_reduce_fusion.2
  306.3 8.2 %collective-permute-done = bf16[128,1024]{1,0:T(8,128)(2,1)S(1)} collective-permute-done((bf16[128,1024]{1,0:T(8,128)(2,1)S(1)}, bf16[128,1024]{1,0:T(8,128)(2,1)S(1)}, u32[]{:S(2)}, u32[]{:S(2)}) %collective-permute-start) | collective-permute-done | bytes 262176 | tf_op jit(solution)/shard_map/ppermute | solution.py:113
  314.5 0.1 fusion.25
  314.6 8.6 %collective-permute-done.1 = bf16[128,1024]{1,0:T(8,128)(2,1)S(1)} collective-permute-done((bf16[128,1024]{1,0:T(8,128)(2,1)S(1)}, bf16[128,1024]{1,0:T(8,128)(2,1)S(1)}, u32[]{:S(2)}, u32[]{:S(2)}) %collective-permute-start.1) | collective-permute-done | bytes 262176 | tf_op jit(solution)/shard_map/ppermute | solution.py:113
  323.3 0.3 multiply_cosine_fusion
  323.6 7.8 %collective-permute-done.2 = bf16[128,1024]{1,0:T(8,128)(2,1)S(1)} collective-permute-done((bf16[128,1024]{1,0:T(8,128)(2,1)S(1)}, bf16[128,1024]{1,0:T(8,128)(2,1)S(1)}, u32[]{:S(2)}, u32[]{:S(2)}) %collective-permute-start.2) | collective-permute-done | bytes 262176 | tf_op jit(solution)/shard_map/ppermute | solution.py:113
  331.6 0.2 convert_reduce_fusion
  331.9 0.4 fusion.11
  332.3 0.0 all-gather.9.cloned.1.call-done
  332.4 2.1 fusion.40
  334.5 0.1 reshape.263
  334.5 0.0 all-gather.11.cloned.1.call-done
  334.6 4.7 %convolution_bitcast_fusion = f32[16,8,8,128]{3,1,2,0:T(8,128)S(1)} fusion(bf16[4096,1024]{1,0:T(8,128)(2,1)} %all-gather.11.cloned.1.call-done, f32[4096]{0:T(1024)S(1)} %convert_element_type.80, f32[128]{0:T(128)S(1)} %add_rsqrt_fusion, f32[128]{0:T(128)S(1)} %broadcast_multiply_fusion.1, bf16[128,8192]{1,0:T(8,128)(2,1)S(1)} %constant_dynamic-update-slice_fusion, ...), kind=kOutput, calls=%fused_computation.27 | convolution fusion | flops 1076363264 | bytes 9978884 | tf_op jit(solution)/shard_map/dot_general | solution.py:118
  339.3 0.1 copy.54
  339.4 0.3 subtract_convert_fusion
  339.6 0.1 pad_maximum_fusion
  339.8 0.2 fusion.43
  340.1 0.4 fusion.44
  340.5 0.3 fusion.22
  340.8 2.1 convolution_convert_fusion.1
  342.9 0.1 copy.50
  343.0 0.3 convolution_convert_fusion
  343.3 0.9 copy.46
  (45 shorter events, 0.5 us)
Async XLA Ops:
  8.0 33.1 %all-gather.5.cloned.1.call-start = ((), (), s32[]{:S(2)}) async-start(), calls=%async_computation.3 | async-start | bytes 1310720 | tf_op jit(solution)/shard_map/all_gather | solution.py:81
  8.7 263.5 %reduce-scatter.2.cloned.1.call-start = ((), (), s32[]{:S(2)}) async-start(), calls=%async_computation.4 | async-start | bytes 10485760 | tf_op jit(solution)/shard_map/reduce_scatter | solution.py:99
  41.1 3.2 copy-start
  101.1 1.9 copy-start.1
  129.0 203.4 %all-gather.9.cloned.1.call-start = ((), (), s32[]{:S(2)}) async-start(), calls=%async_computation.6 | async-start | bytes 2621440 | tf_op jit(solution)/shard_map/all_gather | solution.py:125
  129.5 205.0 %all-gather.11.cloned.1.call-start = ((), (), s32[]{:S(2)}) async-start(), calls=%async_computation.7 | async-start | bytes 10485760 | tf_op jit(solution)/shard_map/all_gather | solution.py:120
  272.2 4.0 %copy-start.5 = (s32[128,2]{0,1:T(2,128)S(1)}, s32[128,2]{0,1:T(2,128)}, u32[]{:S(2)}) copy-start(s32[128,2]{0,1:T(2,128)} %param.15) | copy-start | bytes 3076
  272.2 29.4 %all-to-all-start.1 = ((f32[4,128,1024]{2,1,0:T(8,128)}), f32[4,128,1024]{2,1,0:T(8,128)S(1)}, u32[]{:S(2)}, u32[]{:S(2)}) async-start(f32[4,128,1024]{2,1,0:T(8,128)} %bitcast.91), calls=%async_computation.2 | async-start | bytes 4194304 | tf_op jit(solution)/shard_map/all_to_all | solution.py:100
  275.9 64.8 %all-gather.7.cloned.1.call-start = ((), (), s32[]{:S(2)}) async-start(), calls=%async_computation.5 | async-start | bytes 2621440 | tf_op jit(solution)/shard_map/all_gather | solution.py:130
  302.7 2.0 copy-start.3
  303.3 2.7 copy-start.6
  303.3 19.9 %copy-start.4 = (bf16[4096]{0:T(1024)(128)(2,1)S(1)}, bf16[4096]{0:T(1024)(128)(2,1)}, u32[]{:S(2)}) copy-start(bf16[4096]{0:T(1024)(128)(2,1)} %param.20) | copy-start | bytes 24580
  304.8 26.8 %copy-start.2 = (bf16[128,1024]{1,0:T(8,128)(2,1)}, bf16[128,1024]{1,0:T(8,128)(2,1)S(1)}, u32[]{:S(2)}) copy-start(bf16[128,1024]{1,0:T(8,128)(2,1)S(1)} %add_convert_fusion.1) | copy-start | bytes 786436
  304.8 9.7 %collective-permute-start = (bf16[128,1024]{1,0:T(8,128)(2,1)S(1)}, bf16[128,1024]{1,0:T(8,128)(2,1)S(1)}, u32[]{:S(2)}, u32[]{:S(2)}) collective-permute-start(bf16[128,1024]{1,0:T(8,128)(2,1)S(1)} %add_convert_fusion.1), channel_id=1, source_target_pairs={{0,1},{1,2},{2,3},{3,0},{4,5},{5,6},{6,7},{7,4},{8,9},{9,10},{10,1... | collective-permute-start | bytes 786440 | tf_op jit(solution)/shard_map/ppermute | solution.py:113
  314.5 8.7 %collective-permute-start.1 = (bf16[128,1024]{1,0:T(8,128)(2,1)S(1)}, bf16[128,1024]{1,0:T(8,128)(2,1)S(1)}, u32[]{:S(2)}, u32[]{:S(2)}) collective-permute-start(bf16[128,1024]{1,0:T(8,128)(2,1)S(1)} %collective-permute-done), channel_id=1, source_target_pairs={{0,1},{1,2},{2,3},{3,0},{4,5},{5,6},{6,7},{7,4},{8,9},{9,10},{10,1... | collective-permute-start | bytes 786440 | tf_op jit(solution)/shard_map/ppermute | solution.py:113
  323.2 8.2 %collective-permute-start.2 = (bf16[128,1024]{1,0:T(8,128)(2,1)S(1)}, bf16[128,1024]{1,0:T(8,128)(2,1)S(1)}, u32[]{:S(2)}, u32[]{:S(2)}) collective-permute-start(bf16[128,1024]{1,0:T(8,128)(2,1)S(1)} %collective-permute-done.1), channel_id=1, source_target_pairs={{0,1},{1,2},{2,3},{3,0},{4,5},{5,6},{6,7},{7,4},{8,9},{9,10},{10,1... | collective-permute-start | bytes 786440 | tf_op jit(solution)/shard_map/ppermute | solution.py:113
Sparse Core Ops, SparseCore 0:
  10.4 30.6 all-gather.4
  129.1 143.0 reduce-scatter.1
Sparse Core Ops, SparseCore 1:
  131.0 21.0 all-gather.8
  153.5 58.1 all-gather.10
  306.1 21.7 all-gather.6
